TPU v7x, 32 devices: a whole 2x2x4 slice. The times are simulated.
32 devices in a mesh: dp: 2 (over core), ctx: 16 (over z, y, x).
Axes of the slice: x: 2, y: 2, z: 4, core: 2. Of those that a mesh axis runs over, the one named last changes fastest.
Arguments:
- layer_in: bfloat16 [2, 4096, 768], P('dp', 'ctx'), may hold values from -6 to 6
- out_grad: bfloat16 [2, 4096, 768], P('dp', 'ctx'), may hold values from -6 to 6
- first_gain: bfloat16 [768], P('dp'), may hold values from 0.099609375 to 1.8984375
- query_weight: bfloat16 [768, 768], P('dp'), may hold values from -0.21875 to 0.21875
- key_weight: bfloat16 [768, 768], P('dp'), may hold values from -0.21875 to 0.21875
- value_weight: bfloat16 [768, 768], P('dp'), may hold values from -0.21875 to 0.21875
- output_weight: bfloat16 [768, 768], P('dp'), may hold values from -6 to 6
- second_gain: bfloat16 [768], P('dp'), may hold values from 0.099609375 to 1.8984375
- gate_weight: bfloat16 [768, 2048], P('dp'), may hold values from -0.21875 to 0.21875
- up_weight: bfloat16 [768, 2048], P('dp'), may hold values from -0.21875 to 0.21875
- down_weight: bfloat16 [2048, 768], P('dp'), may hold values from -0.125 to 0.125
Outputs:
- layer_out: bfloat16 [2, 4096, 768], P('dp', 'ctx')
- in_grad: bfloat16 [2, 4096, 768], P('dp', 'ctx')
- first_gain_grad: float32 [768], P('dp')
- query_grad: float32 [768, 768], P('dp')
- key_grad: float32 [768, 768], P('dp')
- value_grad: float32 [768, 768], P('dp')
- output_grad: float32 [768, 768], P('dp')
- second_gain_grad: float32 [768], P('dp')
- gate_grad: float32 [768, 2048], P('dp')
- up_grad: float32 [768, 2048], P('dp')
- down_grad: float32 [2048, 768], P('dp')
All inputs are finite; a program needn't handle non-finite values.
Results may differ from a plain program's by a relative error of at most 0.02.
Values may be sent and summed in bfloat16 or wider, within the bound.
No kernel may reach another device: no remote copies, remote signals or barrier semaphores. Data moves between devices by JAX's collectives and lax.ppermute only.
A program may use at most 448 MiB of HBM per device.

v0:
```python
import jax
import jax.numpy as jnp
from jax import lax
from jax.sharding import PartitionSpec as P

HEADS = 12
HEAD_DIM = 64
EPS = 1e-06


def normed(rows, gain):
    return rows * lax.rsqrt(jnp.mean(rows * rows, axis=-1, keepdims=True) + EPS) * gain


def gated(gate, upper):
    return jax.nn.gelu(gate, approximate=True) * upper


def heads_of(rows):
    return rows.reshape(rows.shape[0], HEADS, HEAD_DIM)


def scores_of(query, keys):
    return jnp.einsum(
        "qhd,khd->hqk", heads_of(query), heads_of(keys), preferred_element_type=jnp.float32
    ) * HEAD_DIM ** (-0.5)


def attend(operands):
    query, keys, values = operands
    scores = scores_of(query, keys)
    top = jnp.max(scores, axis=-1, keepdims=True)
    expd = jnp.exp(scores - top)
    total = jnp.sum(expd, axis=-1, keepdims=True)
    probs = (expd / total).astype(jnp.bfloat16)
    mixed = jnp.einsum("hqk,khd->qhd", probs, heads_of(values), preferred_element_type=jnp.float32)
    mixed = mixed.reshape(query.shape[0], HEADS * HEAD_DIM).astype(jnp.bfloat16)
    return (mixed, (top + jnp.log(total))[..., 0])


def back_core(query, keys, values, grad_mix, logsum):
    probs = jnp.exp(scores_of(query, keys) - logsum[..., None])
    grad_prob = jnp.einsum(
        "qhd,khd->hqk", heads_of(grad_mix), heads_of(values), preferred_element_type=jnp.float32
    )
    delta = jnp.sum(grad_prob * probs, axis=-1)
    grad_score = (probs * (grad_prob - delta[..., None])).astype(jnp.bfloat16)
    return (probs, grad_score, delta)


def query_part(grad_score, keys, count):
    grad_query = jnp.einsum(
        "hqk,khd->qhd", grad_score, heads_of(keys), preferred_element_type=jnp.float32
    ) * HEAD_DIM ** (-0.5)
    return grad_query.reshape(count, HEADS * HEAD_DIM).astype(jnp.bfloat16)


def attend_back(operands):
    query, keys, values, grad_mix, logsum = operands
    probs, grad_score, delta = back_core(query, keys, values, grad_mix, logsum)
    grad_query = query_part(grad_score, keys, query.shape[0])
    grad_keys = jnp.einsum(
        "hqk,qhd->khd", grad_score, heads_of(query), preferred_element_type=jnp.float32
    ) * HEAD_DIM ** (-0.5)
    grad_values = jnp.einsum(
        "hqk,qhd->khd",
        probs.astype(jnp.bfloat16),
        heads_of(grad_mix),
        preferred_element_type=jnp.float32,
    )
    return (
        grad_query,
        grad_keys.reshape(keys.shape[0], -1),
        grad_values.reshape(keys.shape[0], -1),
    )


def product(left, right):
    return jnp.dot(left, right, preferred_element_type=jnp.float32)


def on_device(
    layer_in,
    out_grad,
    first_gain,
    query_weight,
    key_weight,
    value_weight,
    output_weight,
    second_gain,
    gate_weight,
    up_weight,
    down_weight,
):
    seqs, local, width = layer_in.shape
    rows = seqs * local

    def shaped(matrix):
        return matrix.reshape(seqs, local, width)

    gain_one, w_query, w_key, w_value, w_output = (
        lax.all_gather(first_gain, "dp", axis=0, tiled=True),
        lax.all_gather(query_weight, "dp", axis=0, tiled=True),
        lax.all_gather(key_weight, "dp", axis=0, tiled=True),
        lax.all_gather(value_weight, "dp", axis=0, tiled=True),
        lax.all_gather(output_weight, "dp", axis=0, tiled=True),
    )
    inputs = layer_in.reshape(rows, width).astype(jnp.float32)
    gain_one_f = gain_one.astype(jnp.float32)
    normal_one = normed(inputs, gain_one_f).astype(jnp.bfloat16)
    query = product(normal_one, w_query).astype(jnp.bfloat16)
    keys = product(normal_one, w_key).astype(jnp.bfloat16)
    values = product(normal_one, w_value).astype(jnp.bfloat16)
    keys_all, values_all = (
        lax.all_gather(shaped(keys), "ctx", axis=1, tiled=True),
        lax.all_gather(shaped(values), "ctx", axis=1, tiled=True),
    )
    mixed, logsum = lax.map(attend, (shaped(query), keys_all, values_all))
    mixed_rows = mixed.reshape(rows, width)
    middle = inputs + product(mixed_rows, w_output)
    gain_two, w_gate, w_up, w_down = (
        lax.all_gather(second_gain, "dp", axis=0, tiled=True),
        lax.all_gather(gate_weight, "dp", axis=0, tiled=True),
        lax.all_gather(up_weight, "dp", axis=0, tiled=True),
        lax.all_gather(down_weight, "dp", axis=0, tiled=True),
    )
    gain_two_f = gain_two.astype(jnp.float32)
    normal_two = normed(middle, gain_two_f).astype(jnp.bfloat16)
    gate = product(normal_two, w_gate)
    upper = product(normal_two, w_up)
    hidden = gated(gate, upper).astype(jnp.bfloat16)
    result = middle + product(hidden, w_down)
    layer_out = result.astype(jnp.bfloat16).reshape(seqs, local, width)
    gain_one, w_query, w_key, w_value, w_output = (
        lax.all_gather(first_gain, "dp", axis=0, tiled=True),
        lax.all_gather(query_weight, "dp", axis=0, tiled=True),
        lax.all_gather(key_weight, "dp", axis=0, tiled=True),
        lax.all_gather(value_weight, "dp", axis=0, tiled=True),
        lax.all_gather(output_weight, "dp", axis=0, tiled=True),
    )
    gain_two, w_gate, w_up, w_down = (
        lax.all_gather(second_gain, "dp", axis=0, tiled=True),
        lax.all_gather(gate_weight, "dp", axis=0, tiled=True),
        lax.all_gather(up_weight, "dp", axis=0, tiled=True),
        lax.all_gather(down_weight, "dp", axis=0, tiled=True),
    )
    gain_one_f = gain_one.astype(jnp.float32)
    gain_two_f = gain_two.astype(jnp.float32)
    grad_rows = out_grad.reshape(rows, width)
    grad_down = product(hidden.T, grad_rows)
    grad_hidden = product(grad_rows, w_down.T)
    unused, gate_back = jax.vjp(gated, gate, upper)
    grad_gate, grad_upper = gate_back(grad_hidden)
    grad_gate = grad_gate.astype(jnp.bfloat16)
    grad_upper = grad_upper.astype(jnp.bfloat16)
    grad_wgate = product(normal_two.T, grad_gate)
    grad_wup = product(normal_two.T, grad_upper)
    grad_normal_two = product(grad_gate, w_gate.T) + product(grad_upper, w_up.T)
    unused_two, norm_back_two = jax.vjp(normed, middle, gain_two_f)
    grad_middle, grad_gain_two = norm_back_two(grad_normal_two)
    grad_middle = grad_middle + grad_rows.astype(jnp.float32)
    ffn_terms = (
        lax.psum_scatter(
            grad_gain_two.astype(jnp.bfloat16), "dp", scatter_dimension=0, tiled=True
        ).astype(jnp.float32),
        lax.psum_scatter(
            grad_wgate.astype(jnp.bfloat16), "dp", scatter_dimension=0, tiled=True
        ).astype(jnp.float32),
        lax.psum_scatter(
            grad_wup.astype(jnp.bfloat16), "dp", scatter_dimension=0, tiled=True
        ).astype(jnp.float32),
        lax.psum_scatter(
            grad_down.astype(jnp.bfloat16), "dp", scatter_dimension=0, tiled=True
        ).astype(jnp.float32),
    )
    ffn_total = (
        lax.psum(ffn_terms[0].astype(jnp.bfloat16), "ctx").astype(jnp.float32),
        lax.psum(ffn_terms[1].astype(jnp.bfloat16), "ctx").astype(jnp.float32),
        lax.psum(ffn_terms[2].astype(jnp.bfloat16), "ctx").astype(jnp.float32),
        lax.psum(ffn_terms[3].astype(jnp.bfloat16), "ctx").astype(jnp.float32),
    )
    grad_branch = grad_middle.astype(jnp.bfloat16)
    grad_woutput = product(mixed_rows.T, grad_branch)
    grad_mixed = product(grad_branch, w_output.T).astype(jnp.bfloat16)
    grad_query, grad_keys_all, grad_values_all = lax.map(
        attend_back, (shaped(query), keys_all, values_all, shaped(grad_mixed), logsum)
    )
    grad_keys, grad_values = (
        lax.psum_scatter(
            grad_keys_all.astype(jnp.bfloat16), "ctx", scatter_dimension=1, tiled=True
        ).astype(jnp.float32),
        lax.psum_scatter(
            grad_values_all.astype(jnp.bfloat16), "ctx", scatter_dimension=1, tiled=True
        ).astype(jnp.float32),
    )
    grad_keys = grad_keys.astype(jnp.bfloat16)
    grad_values = grad_values.astype(jnp.bfloat16)
    grad_query = grad_query.reshape(rows, width)
    grad_keys = grad_keys.reshape(rows, width)
    grad_values = grad_values.reshape(rows, width)
    grad_wquery = product(normal_one.T, grad_query)
    grad_wkey = product(normal_one.T, grad_keys)
    grad_wvalue = product(normal_one.T, grad_values)
    grad_normal_one = (
        product(grad_query, w_query.T)
        + product(grad_keys, w_key.T)
        + product(grad_values, w_value.T)
    )
    unused_one, norm_back_one = jax.vjp(normed, inputs, gain_one_f)
    grad_inputs, grad_gain_one = norm_back_one(grad_normal_one)
    in_grad = (grad_inputs + grad_middle).astype(jnp.bfloat16).reshape(seqs, local, width)
    attn_terms = (
        lax.psum_scatter(
            grad_gain_one.astype(jnp.bfloat16), "dp", scatter_dimension=0, tiled=True
        ).astype(jnp.float32),
        lax.psum_scatter(
            grad_wquery.astype(jnp.bfloat16), "dp", scatter_dimension=0, tiled=True
        ).astype(jnp.float32),
        lax.psum_scatter(
            grad_wkey.astype(jnp.bfloat16), "dp", scatter_dimension=0, tiled=True
        ).astype(jnp.float32),
        lax.psum_scatter(
            grad_wvalue.astype(jnp.bfloat16), "dp", scatter_dimension=0, tiled=True
        ).astype(jnp.float32),
        lax.psum_scatter(
            grad_woutput.astype(jnp.bfloat16), "dp", scatter_dimension=0, tiled=True
        ).astype(jnp.float32),
    )
    attn_total = (
        lax.psum(attn_terms[0].astype(jnp.bfloat16), "ctx").astype(jnp.float32),
        lax.psum(attn_terms[1].astype(jnp.bfloat16), "ctx").astype(jnp.float32),
        lax.psum(attn_terms[2].astype(jnp.bfloat16), "ctx").astype(jnp.float32),
        lax.psum(attn_terms[3].astype(jnp.bfloat16), "ctx").astype(jnp.float32),
        lax.psum(attn_terms[4].astype(jnp.bfloat16), "ctx").astype(jnp.float32),
    )
    return (
        layer_out,
        in_grad,
        attn_total[0],
        attn_total[1],
        attn_total[2],
        attn_total[3],
        attn_total[4],
        ffn_total[0],
        ffn_total[1],
        ffn_total[2],
        ffn_total[3],
    )


def solution(mesh):
    in_specs = (
        P("dp", "ctx", None),
        P("dp", "ctx", None),
        P("dp"),
        P("dp", None),
        P("dp", None),
        P("dp", None),
        P("dp", None),
        P("dp"),
        P("dp", None),
        P("dp", None),
        P("dp", None),
    )
    out_specs = (
        P("dp", "ctx", None),
        P("dp", "ctx", None),
        P("dp"),
        P("dp", None),
        P("dp", None),
        P("dp", None),
        P("dp", None),
        P("dp"),
        P("dp", None),
        P("dp", None),
        P("dp", None),
    )
    return jax.shard_map(
        on_device, mesh=mesh, in_specs=in_specs, out_specs=out_specs, check_vma=False
    )
```

profile of v0, /device:TPU:0, one launch (start us, length us, event | category | flops | bytes accessed | tf_op | source)
XLA Modules:
  0.0 1049.3 jit_solution(17920821551046934564)
XLA Ops:
  13.8 7.7 all-gather.18.cloned.1.call-done
  24.3 9.2 all-gather.14.cloned.1.call-done
  40.8 4.7 all-gather.16.cloned.1.call-done
  47.5 96.6 %all-gather.30.cloned.1.call-done = bf16[4096,768]{1,0:T(8,128)(2,1)} async-done(((bf16[256,768]{1,0:T(8,128)(2,1)}), bf16[4096,768]{1,0:T(8,128)(2,1)}) %all-gather.30.cloned.1.call-update) | async-done | bytes 6291472 | tf_op jit(solution)/shard_map/all_gather | solution.py:115
  144.0 8.7 copy.36
  152.7 22.9 %multiply_reduce_fusion.1 = (f32[12,256]{1,0:T(8,128)S(1)}, f32[12,256,4096]{2,1,0:T(8,128)}) fusion(bf16[256,12,64]{0,2,1:T(8,128)(2,1)S(1)} %bitcast.127, bf16[4096,12,64]{0,2,1:T(8,128)(2,1)} %bitcast.119), kind=kOutput, calls=%fused_computation.6 | convolution fusion | flops 1635775488 | bytes 57028608 | tf_op jit(solution)/shard_map/while/body/eval_jaxpr/qhd,khd->hqk/dot_general | solution.py:24
  175.7 20.5 %fusion = f32[12,256]{1,0:T(8,128)S(1)} fusion(f32[12,256,4096]{2,1,0:T(8,128)} %get-tuple-element.75, f32[12,256]{1,0:T(8,128)S(1)} %get-tuple-element.74), kind=kLoop, calls=%fused_computation.5 | loop fusion | flops 37745664 | bytes 50356224 | tf_op jit(solution)/shard_map/while/body/eval_jaxpr/reduce_sum | solution.py:34
  196.2 43.5 %all-gather.28.cloned.1.call-done = bf16[4096,768]{1,0:T(8,128)(2,1)} async-done(((bf16[256,768]{1,0:T(8,128)(2,1)}), bf16[4096,768]{1,0:T(8,128)(2,1)}) %all-gather.28.cloned.1.call-update) | async-done | bytes 6291472 | tf_op jit(solution)/shard_map/all_gather | solution.py:116
  239.7 8.7 copy.34
  248.4 22.0 %fusion.19 = bf16[12,64,256]{2,1,0:T(8,128)(2,1)S(1)} fusion(bf16[4096,12,64]{0,2,1:T(8,128)(2,1)} %bitcast.121, f32[12,256,4096]{2,1,0:T(8,128)} %get-tuple-element.75, f32[12,256]{1,0:T(8,128)S(1)} %fusion, f32[12,256]{1,0:T(8,128)S(1)} %get-tuple-element.74), kind=kOutput, calls=%fused_computation.45 | convolution fusion | flops 1661140992 | bytes 57040896 | tf_op jit(solution)/shard_map/while/body/eval_jaxpr/hqk,khd->qhd/dot_general | solution.py:36
  272.6 4.6 fusion.57
  278.5 4.2 fusion.58
  282.7 10.7 %all-gather.26.cloned.1.call-done = bf16[2048,768]{1,0:T(8,128)(2,1)} async-done(((bf16[1024,768]{1,0:T(8,128)(2,1)}), bf16[2048,768]{1,0:T(8,128)(2,1)}) %all-gather.26.cloned.1.call-update) | async-done | bytes 3145744 | tf_op jit(solution)/shard_map/all_gather | solution.py:125
  293.3 6.9 multiply_convert_fusion.2
  305.6 35.5 %multiply_reduce_fusion = (f32[12,256]{1,0:T(8,128)}, f32[12,256,4096]{2,1,0:T(8,128)}) fusion(f32[12,256,4096]{2,1,0:T(8,128)} %get-tuple-element.75, f32[12,256]{1,0:T(8,128)S(1)} %log_add_fusion, bf16[256,12,64]{0,2,1:T(8,128)(2,1)S(1)} %bitcast.125, bf16[4096,12,64]{0,2,1:T(8,128)(2,1)} %bitcast.122), kind=kOutput, calls=%fused_computation.1 | convolution fusion | flops 1660941312 | bytes 107372544 | tf_op jit(solution)/shard_map/while/body/eval_jaxpr/qhd,khd->hqk/dot_general | solution.py:43
  341.1 40.2 %multiply_convert_fusion = bf16[12,256,4096]{2,1,0:T(8,128)(2,1)} fusion(f32[12,256,4096]{2,1,0:T(8,128)} %get-tuple-element.80, f32[12,256,4096]{2,1,0:T(8,128)} %get-tuple-element.75, f32[12,256]{1,0:T(8,128)} %get-tuple-element.79, f32[12,256]{1,0:T(8,128)S(1)} %log_add_fusion), kind=kLoop, calls=%fused_computation | loop fusion | flops 62914560 | bytes 125853696 | tf_op jit(solution)/shard_map/while/body/eval_jaxpr/convert_element_type | solution.py:47
  381.3 15.2 %multiply_convert_fusion.1 = bf16[12,64,4096]{2,1,0:T(8,128)(2,1)} fusion(bf16[256,12,64]{0,2,1:T(8,128)(2,1)S(1)} %bitcast.128, bf16[12,256,4096]{2,1,0:T(8,128)(2,1)} %multiply_convert_fusion), kind=kOutput, calls=%fused_computation.12 | convolution fusion | flops 1616904192 | bytes 31850496 | tf_op jit(solution)/shard_map/while/body/eval_jaxpr/hqk,qhd->khd/dot_general | solution.py:62
  396.6 22.0 %fusion.7 = bf16[12,64,4096]{2,1,0:T(8,128)(2,1)} fusion(bf16[256,12,64]{0,2,1:T(8,128)(2,1)S(1)} %bitcast.126, f32[12,256,4096]{2,1,0:T(8,128)} %get-tuple-element.75, f32[12,256]{1,0:T(8,128)S(1)} %log_add_fusion), kind=kOutput, calls=%fused_computation.13 | convolution fusion | flops 1651507200 | bytes 57028608 | tf_op jit(solution)/shard_map/while/body/eval_jaxpr/hqk,qhd->khd/dot_general | solution.py:65
  418.6 14.4 %fusion.18 = bf16[12,64,256]{2,1,0:T(8,128)(2,1)S(1)} fusion(bf16[4096,12,64]{0,2,1:T(8,128)(2,1)} %bitcast.120, bf16[12,256,4096]{2,1,0:T(8,128)(2,1)} %multiply_convert_fusion), kind=kOutput, calls=%fused_computation.44 | convolution fusion | flops 1611005952 | bytes 31850496 | tf_op jit(solution)/shard_map/while/body/eval_jaxpr/hqk,khd->qhd/dot_general | solution.py:52
  436.4 3.9 convolution_convert_fusion.2
  448.3 95.9 %reduce-scatter.10.cloned.1.call-done = bf16[1,256,768]{1,2,0:T(8,128)(2,1)} async-done(((bf16[1,4096,768]{1,2,0:T(8,128)(2,1)}), bf16[1,256,768]{1,2,0:T(8,128)(2,1)}) %reduce-scatter.10.cloned.1.call-update) | async-done | bytes 393232 | tf_op jit(solution)/shard_map/reduce_scatter | solution.py:189
  546.9 148.6 %reduce-scatter.12.cloned.1.call-done = bf16[1,256,768]{1,2,0:T(8,128)(2,1)} async-done(((bf16[1,4096,768]{1,2,0:T(8,128)(2,1)}), bf16[1,256,768]{1,2,0:T(8,128)(2,1)}) %reduce-scatter.12.cloned.1.call-update) | async-done | bytes 393232 | tf_op jit(solution)/shard_map/reduce_scatter | solution.py:192
  698.4 7.6 reduce-scatter.14.cloned.1.call-done
  706.0 12.8 %reduce-scatter.20.cloned.1.call-done = bf16[384,768]{1,0:T(8,128)(2,1)} async-done(((bf16[768,768]{1,0:T(8,128)(2,1)}), bf16[384,768]{1,0:T(8,128)(2,1)}) %reduce-scatter.20.cloned.1.call-update) | async-done | bytes 589840 | tf_op jit(solution)/shard_map/reduce_scatter | solution.py:225
  718.8 14.8 %reduce-scatter.22.cloned.1.call-done = bf16[384,2048]{1,0:T(8,128)(2,1)} async-done(((bf16[768,2048]{1,0:T(8,128)(2,1)}), bf16[384,2048]{1,0:T(8,128)(2,1)}) %reduce-scatter.22.cloned.1.call-update) | async-done | bytes 1572880 | tf_op jit(solution)/shard_map/reduce_scatter | solution.py:166
  733.6 14.9 %reduce-scatter.24.cloned.1.call-done = bf16[384,2048]{1,0:T(8,128)(2,1)} async-done(((bf16[768,2048]{1,0:T(8,128)(2,1)}), bf16[384,2048]{1,0:T(8,128)(2,1)}) %reduce-scatter.24.cloned.1.call-update) | async-done | bytes 1572880 | tf_op jit(solution)/shard_map/reduce_scatter | solution.py:169
  748.4 14.8 %reduce-scatter.26.cloned.1.call-done = bf16[1024,768]{1,0:T(8,128)(2,1)} async-done(((bf16[2048,768]{1,0:T(8,128)(2,1)}), bf16[1024,768]{1,0:T(8,128)(2,1)}) %reduce-scatter.26.cloned.1.call-update) | async-done | bytes 1572880 | tf_op jit(solution)/shard_map/reduce_scatter | solution.py:172
  763.2 12.6 %reduce-scatter.16.cloned.1.call-done = bf16[384,768]{1,0:T(8,128)(2,1)} async-done(((bf16[768,768]{1,0:T(8,128)(2,1)}), bf16[384,768]{1,0:T(8,128)(2,1)}) %reduce-scatter.16.cloned.1.call-update) | async-done | bytes 589840 | tf_op jit(solution)/shard_map/reduce_scatter | solution.py:219
  775.8 12.6 %reduce-scatter.18.cloned.1.call-done = bf16[384,768]{1,0:T(8,128)(2,1)} async-done(((bf16[768,768]{1,0:T(8,128)(2,1)}), bf16[384,768]{1,0:T(8,128)(2,1)}) %reduce-scatter.18.cloned.1.call-update) | async-done | bytes 589840 | tf_op jit(solution)/shard_map/reduce_scatter | solution.py:222
  792.1 3.8 fusion.20
  799.8 43.9 %all-reduce.2 = (bf16[384]{0:T(512)(128)(2,1)S(1)}, bf16[384]{0:T(512)(128)(2,1)S(1)}) all-reduce(bf16[384]{0:T(512)(128)(2,1)S(1)} %dynamic-slice.3, bf16[384]{0:T(512)(128)(2,1)S(1)} %dynamic-slice.5), channel_id=1, replica_groups=mesh['dp'=2,'ctx'=16] {'ctx'}, use_global_device_ids=true, to_apply=%region_11.12 | all-reduce | flops 768 | bytes 3072 | tf_op jit(solution)/shard_map/psum | solution.py:230
  845.9 184.0 %all-reduce.7.cloned.1.call-done = (bf16[384,768]{1,0:T(8,128)(2,1)}, bf16[384,768]{1,0:T(8,128)(2,1)}, bf16[384,768]{1,0:T(8,128)(2,1)}, bf16[384,768]{1,0:T(8,...) async-done(((bf16[384,768]{1,0:T(8,128)(2,1)}, bf16[384,768]{1,0:T(8,128)(2,1)}, bf16[384,768]{1,0:T(8,128)(2,1)}, ...) | async-done | bytes 7077904 | tf_op jit(solution)/shard_map/psum | solution.py:231
  (153 shorter events, 65.7 us)
Async XLA Ops:
  7.2 26.3 %copy-start = (bf16[1,256,768]{2,1,0:T(8,128)(2,1)S(1)}, bf16[1,256,768]{2,1,0:T(8,128)(2,1)}, u32[]{:S(2)}) copy-start(bf16[1,256,768]{2,1,0:T(8,128)(2,1)} %param.11) | copy-start | bytes 1179652
  7.2 14.3 %all-gather.18.cloned.1.call-start = ((), (), s32[]{:S(2)}) async-start(), calls=%async_computation.11 | async-start | bytes 1769472 | tf_op jit(solution)/shard_map/all_gather | solution.py:104
  7.9 25.6 %all-gather.14.cloned.1.call-start = ((), (), s32[]{:S(2)}) async-start(), calls=%async_computation.9 | async-start | bytes 1769472 | tf_op jit(solution)/shard_map/all_gather | solution.py:105
  8.7 36.8 %all-gather.16.cloned.1.call-start = ((), (), s32[]{:S(2)}) async-start(), calls=%async_computation.10 | async-start | bytes 1769472 | tf_op jit(solution)/shard_map/all_gather | solution.py:103
  9.4 134.6 %all-gather.30.cloned.1.call-start = ((), (), s32[]{:S(2)}) async-start(), calls=%async_computation.26 | async-start | bytes 6684672 | tf_op jit(solution)/shard_map/all_gather | solution.py:115
  12.1 33.4 %copy-start.23 = (f32[768]{0:T(1024)}, f32[768]{0:T(1024)S(1)}, u32[]{:S(2)}) copy-start(f32[768]{0:T(1024)S(1)} %reshape.240) | copy-start | bytes 9220
  13.8 31.6 %copy-start.25 = (f32[256]{0:T(256)}, f32[256]{0:T(256)S(1)}, u32[]{:S(2)}) copy-start(f32[256]{0:T(256)S(1)} %fusion.47) | copy-start | bytes 3076
  24.2 215.5 %all-gather.28.cloned.1.call-start = ((), (), s32[]{:S(2)}) async-start(), calls=%async_computation.25 | async-start | bytes 6684672 | tf_op jit(solution)/shard_map/all_gather | solution.py:116
  36.1 234.4 %all-gather.20.cloned.1.call-start = ((), (), s32[]{:S(2)}) async-start(), calls=%async_computation.12 | async-start | bytes 1769472 | tf_op jit(solution)/shard_map/all_gather | solution.py:106
  36.6 235.9 %all-gather.22.cloned.1.call-start = ((), (), s32[]{:S(2)}) async-start(), calls=%async_computation.13 | async-start | bytes 4718592 | tf_op jit(solution)/shard_map/all_gather | solution.py:123
  37.4 241.1 %all-gather.24.cloned.1.call-start = ((), (), s32[]{:S(2)}) async-start(), calls=%async_computation.14 | async-start | bytes 4718592 | tf_op jit(solution)/shard_map/all_gather | solution.py:124
  38.1 255.2 %all-gather.26.cloned.1.call-start = ((), (), s32[]{:S(2)}) async-start(), calls=%async_computation.15 | async-start | bytes 4718592 | tf_op jit(solution)/shard_map/all_gather | solution.py:125
  38.9 505.3 %reduce-scatter.10.cloned.1.call-start = ((), (), s32[]{:S(2)}) async-start(), calls=%async_computation.16 | async-start | bytes 6684672 | tf_op jit(solution)/shard_map/reduce_scatter | solution.py:189
  47.4 105.3 %copy-start.3 = (bf16[256,768]{0,1:T(8,128)(2,1)}, bf16[256,768]{0,1:T(8,128)(2,1)S(1)}, u32[]{:S(2)}) copy-start(bf16[256,768]{0,1:T(8,128)(2,1)S(1)} %copy.35) | copy-start | bytes 1179652
  277.2 16.1 %copy-start.11 = (bf16[1,256,768]{2,1,0:T(8,128)(2,1)S(1)}, bf16[1,256,768]{2,1,0:T(8,128)(2,1)}, u32[]{:S(2)}) copy-start(bf16[1,256,768]{2,1,0:T(8,128)(2,1)} %param.12) | copy-start | bytes 1179652
  293.3 7.0 copy-start.10
  341.1 40.2 %copy-start.4 = (bf16[256,768]{0,1:T(8,128)(2,1)S(1)}, bf16[256,768]{0,1:T(8,128)(2,1)}, u32[]{:S(2)}) copy-start(bf16[256,768]{0,1:T(8,128)(2,1)} %copy-done.3) | copy-start | bytes 1179652
  396.5 299.0 %reduce-scatter.12.cloned.1.call-start = ((), (), s32[]{:S(2)}) async-start(), calls=%async_computation.17 | async-start | bytes 6684672 | tf_op jit(solution)/shard_map/reduce_scatter | solution.py:192
  418.6 14.5 %copy-start.24 = (f32[768]{0:T(1024)S(1)}, f32[768]{0:T(1024)}, u32[]{:S(2)}) copy-start(f32[768]{0:T(1024)} %copy-done.23) | copy-start | bytes 9220
  418.6 14.5 %copy-start.26 = (f32[256]{0:T(256)S(1)}, f32[256]{0:T(256)}, u32[]{:S(2)}) copy-start(f32[256]{0:T(256)} %copy-done.25) | copy-start | bytes 3076
  418.6 287.4 %reduce-scatter.14.cloned.1.call-start = ((), (), s32[]{:S(2)}) async-start(), calls=%async_computation.18 | async-start | bytes 1769472 | tf_op jit(solution)/shard_map/reduce_scatter | solution.py:216
  434.7 284.0 %reduce-scatter.20.cloned.1.call-start = ((), (), s32[]{:S(2)}) async-start(), calls=%async_computation.21 | async-start | bytes 1769472 | tf_op jit(solution)/shard_map/reduce_scatter | solution.py:225
  436.3 297.2 %reduce-scatter.22.cloned.1.call-start = ((), (), s32[]{:S(2)}) async-start(), calls=%async_computation.22 | async-start | bytes 4718592 | tf_op jit(solution)/shard_map/reduce_scatter | solution.py:166
  440.3 308.1 %reduce-scatter.24.cloned.1.call-start = ((), (), s32[]{:S(2)}) async-start(), calls=%async_computation.23 | async-start | bytes 4718592 | tf_op jit(solution)/shard_map/reduce_scatter | solution.py:169
  444.2 318.9 %reduce-scatter.26.cloned.1.call-start = ((), (), s32[]{:S(2)}) async-start(), calls=%async_computation.24 | async-start | bytes 4718592 | tf_op jit(solution)/shard_map/reduce_scatter | solution.py:172
  448.3 327.5 %reduce-scatter.16.cloned.1.call-start = ((), (), s32[]{:S(2)}) async-start(), calls=%async_computation.19 | async-start | bytes 1769472 | tf_op jit(solution)/shard_map/reduce_scatter | solution.py:219
  546.8 241.5 %reduce-scatter.18.cloned.1.call-start = ((), (), s32[]{:S(2)}) async-start(), calls=%async_computation.20 | async-start | bytes 1769472 | tf_op jit(solution)/shard_map/reduce_scatter | solution.py:222
  698.1 331.8 %all-reduce.7.cloned.1.call-start = ((), (), s32[]{:S(2)}) async-start(), calls=%async_computation.27 | async-start | bytes 14155776 | tf_op jit(solution)/shard_map/psum | solution.py:231
  795.9 49.0 %copy-start.28 = (f32[256]{0:T(256)S(1)}, f32[256]{0:T(256)}, u32[]{:S(2)}) copy-start(f32[256]{0:T(256)} %copy-done.27) | copy-start | bytes 3076
  1029.9 4.5 copy-start.22
  1029.9 5.6 copy-start.21
  1029.9 6.7 copy-start.17
  (19 other events, 49.2 us)
Sparse Core Ops, SparseCore 0:
  9.6 11.9 all-gather.17
  23.1 10.3 all-gather.13
  35.0 10.3 all-gather.15
  48.7 95.2 all-gather.29
  147.2 92.4 all-gather.27
  241.1 7.4 all-gather.19
  250.2 13.2 all-gather.21
  265.0 13.3 all-gather.23
  280.0 13.2 all-gather.25
  396.6 147.5 reduce-scatter.9
  549.4 146.0 reduce-scatter.11
  698.1 7.7 reduce-scatter.13
  708.9 9.8 reduce-scatter.19
  721.4 12.0 reduce-scatter.21
  736.3 12.0 reduce-scatter.23
  751.1 12.0 reduce-scatter.25
  765.9 9.8 reduce-scatter.15
  778.5 9.8 reduce-scatter.17
  795.9 233.8 all-reduce.6
where the time goes:
time: 1060 us; the launch traced here: 1050 us
  waiting for transfers between devices  697 us (66%)
  matrix products  184 us (17%)
  other arithmetic  77.1 us (7%)
  blocking collectives  50.1 us (5%)
  local copies, waits for them, and re-layouts  24.6 us (2%)
  between operations  15.3 us (1%)
    psum x1, waiting for transfers between devices, on_device(): lax.psum(attn_terms[1].astype(jnp.bfloat16), 'ctx').astype(jnp.float32)  184 us
    reduce_scatter x1, waiting for transfers between devices, on_device(): lax.psum_scatter(grad_values_all.astype(jnp.bfloat16), 'ctx', scatter_dim...  149 us
    all_gather x1, waiting for transfers between devices, on_device(): lax.all_gather(shaped(keys), 'ctx', axis=1, tiled=True)  96.6 us
    reduce_scatter x1, waiting for transfers between devices, on_device(): lax.psum_scatter(grad_keys_all.astype(jnp.bfloat16), 'ctx', scatter_dimen...  95.9 us
    dot_general x21, matrix products, product(): return jnp.dot(left, right, preferred_element_type=jnp.float32)  52.2 us
    psum x1, blocking collectives, on_device(): lax.psum(attn_terms[0].astype(jnp.bfloat16), 'ctx').astype(jnp.float32)  43.9 us
    all_gather x1, waiting for transfers between devices, on_device(): lax.all_gather(shaped(values), 'ctx', axis=1, tiled=True)  43.5 us
    convert_element_type x1, other arithmetic, back_core(): grad_score = (probs * (grad_prob - delta[..., None])).astype(jnp.bfloat16)  40.2 us
  transfers between devices with their start and end apart: 19, of which 17 were waited for; matrix products, arithmetic and copies ran while one was open for 16% of the time, Pallas kernels for 0%

commit v1 on v0

--- a/solution.py
+++ b/solution.py
@@ -6,6 +6,28 @@
 HEADS = 12
 HEAD_DIM = 64
 EPS = 1e-06
+
+
+def laid_out(pieces, dim):
+    lengths = list(pieces.shape[1:])
+    lengths[dim] *= pieces.shape[0]
+    return jnp.moveaxis(pieces, 0, dim).reshape(lengths)
+
+
+def gather_around(x, axis, dim):
+    length = lax.axis_size(axis)
+    pairs = [(i, (i + 1) % length) for i in range(length)]
+    back = [(b, a) for a, b in pairs]
+    lower, upper = ([], [])
+    for step in range(length - 1):
+        if step % 2 == 0:
+            lower.append(lax.ppermute(lower[-1] if lower else x, axis, pairs))
+        else:
+            upper.append(lax.ppermute(upper[-1] if upper else x, axis, back))
+    pieces = jnp.stack([*lower[::-1], x, *upper])
+    shift = lax.axis_index(axis) - len(lower)
+    pieces = pieces[(jnp.arange(length) - shift) % length]
+    return laid_out(pieces, dim)
 
 
 def normed(rows, gain):
@@ -113,7 +135,7 @@
     values = product(normal_one, w_value).astype(jnp.bfloat16)
     keys_all, values_all = (
         lax.all_gather(shaped(keys), "ctx", axis=1, tiled=True),
-        lax.all_gather(shaped(values), "ctx", axis=1, tiled=True),
+        gather_around(shaped(values), "ctx", 1),
     )
     mixed, logsum = lax.map(attend, (shaped(query), keys_all, values_all))
     mixed_rows = mixed.reshape(rows, width)

time: 1060 us -> 1090 us (1.028)
  starting transfers between devices: 0.98 us -> 85.3 us
  waiting for transfers between devices: 697 us -> 617 us
  local copies, waits for them, and re-layouts: 24.6 us -> 58.2 us
    all_gather x1, waiting for transfers between devices: 96.6 us -> 0.01 us  [on_device(): lax.all_gather(shaped(keys), 'ctx', axis=1, tiled=True)]
    ppermute x0 -> x15, starting transfers between devices: none -> 84.4 us  [the longest x7 64.1 us: gather_around(): upper.append(lax.ppermute(upper[-1] if upper else x, axis, back))]
    ppermute x0 -> x15, waiting for transfers between devices: none -> 82.8 us  [the longest x8 73.8 us: gather_around(): lower.append(lax.ppermute(lower[-1] if lower else x, axis, pairs))]
    all_gather x1 -> x0, waiting for transfers between devices: 43.5 us -> none  [on_device(): lax.all_gather(shaped(values), 'ctx', axis=1, tiled=True)]
    gather x0 -> x2, local copies, waits for them, and re-layouts: none -> 15.9 us  [gather_around(): pieces = pieces[(jnp.arange(length) - shift) % length]]
    unnamed x69 -> x86, local copies, waits for them, and re-layouts: 6.81 us -> 21 us
  transfers between devices with their start and end apart: 19 -> 33, of which waited for: 17 -> 23; matrix products, arithmetic and copies ran while one was open for 16% -> 19% of each run, Pallas kernels for 0% -> 0%
where the time goes in v1:
time: 1090 us
  waiting for transfers between devices  617 us (57%)
  matrix products  182 us (17%)
  starting transfers between devices  85.3 us (8%)
  other arithmetic  80.7 us (7%)
  local copies, waits for them, and re-layouts  58.2 us (5%)
  blocking collectives  50.1 us (5%)
  between operations  15.7 us (1%)
    psum x1, waiting for transfers between devices, on_device(): lax.psum(attn_terms[1].astype(jnp.bfloat16), 'ctx').astype(jnp.float32)  184 us
    reduce_scatter x1, waiting for transfers between devices, on_device(): lax.psum_scatter(grad_values_all.astype(jnp.bfloat16), 'ctx', scatter_dim...  148 us
    reduce_scatter x1, waiting for transfers between devices, on_device(): lax.psum_scatter(grad_keys_all.astype(jnp.bfloat16), 'ctx', scatter_dimen...  92.5 us
    ppermute x8, waiting for transfers between devices, gather_around(): lower.append(lax.ppermute(lower[-1] if lower else x, axis, pairs))  73.8 us
    ppermute x7, starting transfers between devices, gather_around(): upper.append(lax.ppermute(upper[-1] if upper else x, axis, back))  64.1 us
    dot_general x21, matrix products, product(): return jnp.dot(left, right, preferred_element_type=jnp.float32)  53.5 us
    psum x1, blocking collectives, on_device(): lax.psum(attn_terms[0].astype(jnp.bfloat16), 'ctx').astype(jnp.float32)  44 us
    convert_element_type x1, other arithmetic, back_core(): grad_score = (probs * (grad_prob - delta[..., None])).astype(jnp.bfloat16)  40.1 us
  transfers between devices with their start and end apart: 33, of which 23 were waited for; matrix products, arithmetic and copies ran while one was open for 19% of the time, Pallas kernels for 0%

profile of v1, /device:TPU:0, one launch (start us, length us, event | category | flops | bytes accessed | tf_op | source)
XLA Modules:
  0.0 1088.5 jit_solution(3382366581399136043)
XLA Ops:
  13.3 8.2 all-gather.16.cloned.1.call-done
  37.1 13.3 %collective-permute-done = bf16[1,256,768]{2,1,0:T(8,128)(2,1)S(1)} collective-permute-done((bf16[1,256,768]{2,1,0:T(8,128)(2,1)S(1)}, bf16[1,256,768]{2,1,0:T(8,128)(2,1)S(1)}, u32[]{:S(2)}, u32[]{:S(2)}) %collective-permute-start) | collective-permute-done | bytes 393248 | tf_op jit(solution)/shard_map/ppermute | solution.py:24
  55.9 14.0 %collective-permute-done.1 = bf16[1,256,768]{2,1,0:T(8,128)(2,1)S(1)} collective-permute-done((bf16[1,256,768]{2,1,0:T(8,128)(2,1)S(1)}, bf16[1,256,768]{2,1,0:T(8,128)(2,1)S(1)}, u32[]{:S(2)}, u32[]{:S(2)}) %collective-permute-start.1) | collective-permute-done | bytes 393248 | tf_op jit(solution)/shard_map/ppermute | solution.py:24
  72.4 16.4 %collective-permute-start.9 = (bf16[1,256,768]{2,1,0:T(8,128)(2,1)S(1)}, bf16[1,256,768]{2,1,0:T(8,128)(2,1)S(1)}, u32[]{:S(2)}, u32[]{:S(2)}) collective-permute-start(bf16[1,256,768]{2,1,0:T(8,128)(2,1)S(1)} %collective-permute-done.8), channel_id=1, source_target_pairs={{1,0},{2,1},{3,2},{4,3},{5,4},{6,5},{7,6},{8,7},{9,8},{10,9},{11,1... | collective-permute-start | bytes 1179656 | tf_op jit(solution)/shard_map/ppermute | solution.py:26
  88.8 10.9 collective-permute-done.2
  104.5 11.4 %collective-permute-start.10 = (bf16[1,256,768]{2,1,0:T(8,128)(2,1)S(1)}, bf16[1,256,768]{2,1,0:T(8,128)(2,1)S(1)}, u32[]{:S(2)}, u32[]{:S(2)}) collective-permute-start(bf16[1,256,768]{2,1,0:T(8,128)(2,1)S(1)} %collective-permute-done.9), channel_id=1, source_target_pairs={{1,0},{2,1},{3,2},{4,3},{5,4},{6,5},{7,6},{8,7},{9,8},{10,9},{11,1... | collective-permute-start | bytes 1179656 | tf_op jit(solution)/shard_map/ppermute | solution.py:26
  129.4 11.1 %collective-permute-done.4 = bf16[1,256,768]{2,1,0:T(8,128)(2,1)S(1)} collective-permute-done((bf16[1,256,768]{2,1,0:T(8,128)(2,1)S(1)}, bf16[1,256,768]{2,1,0:T(8,128)(2,1)S(1)}, u32[]{:S(2)}, u32[]{:S(2)}) %collective-permute-start.4) | collective-permute-done | bytes 393248 | tf_op jit(solution)/shard_map/ppermute | solution.py:24
  146.2 9.5 collective-permute-start.12
  155.7 11.5 %collective-permute-done.5 = bf16[1,256,768]{2,1,0:T(8,128)(2,1)} collective-permute-done((bf16[1,256,768]{2,1,0:T(8,128)(2,1)S(1)}, bf16[1,256,768]{2,1,0:T(8,128)(2,1)}, u32[]{:S(2)}, u32[]{:S(2)}) %collective-permute-start.5) | collective-permute-done | bytes 393248 | tf_op jit(solution)/shard_map/ppermute | solution.py:24
  175.5 8.5 collective-permute-start.13
  235.9 9.6 copy.34
  245.5 10.5 reshape.271
  256.0 8.6 copy.36
  264.6 22.2 %multiply_reduce_fusion.1 = (f32[12,256]{1,0:T(8,128)S(1)}, f32[12,256,4096]{2,1,0:T(8,128)}) fusion(bf16[256,12,64]{0,2,1:T(8,128)(2,1)S(1)} %bitcast.162, bf16[4096,12,64]{0,2,1:T(8,128)(2,1)} %bitcast.156), kind=kOutput, calls=%fused_computation.7 | convolution fusion | flops 1635775488 | bytes 57028608 | tf_op jit(solution)/shard_map/while/body/eval_jaxpr/qhd,khd->hqk/dot_general | solution.py:46
  286.8 20.8 %fusion = f32[12,256]{1,0:T(8,128)S(1)} fusion(f32[12,256,4096]{2,1,0:T(8,128)} %get-tuple-element.75, f32[12,256]{1,0:T(8,128)S(1)} %get-tuple-element.74), kind=kLoop, calls=%fused_computation.6 | loop fusion | flops 37745664 | bytes 50356224 | tf_op jit(solution)/shard_map/while/body/eval_jaxpr/reduce_sum | solution.py:56
  307.6 19.2 %fusion.19 = bf16[12,64,256]{2,1,0:T(8,128)(2,1)S(1)} fusion(bf16[4096,12,64]{0,2,1:T(8,128)(2,1)S(1)} %copy-done, f32[12,256,4096]{2,1,0:T(8,128)} %get-tuple-element.75, f32[12,256]{1,0:T(8,128)S(1)} %fusion, f32[12,256]{1,0:T(8,128)S(1)} %get-tuple-element.74), kind=kOutput, calls=%fused_computation.46 | convolution fusion | flops 1661140992 | bytes 57040896 | tf_op jit(solution)/shard_map/while/body/eval_jaxpr/hqk,khd->qhd/dot_general | solution.py:58
  347.4 35.0 %multiply_reduce_fusion = (f32[12,256]{1,0:T(8,128)S(1)}, f32[12,256,4096]{2,1,0:T(8,128)}) fusion(f32[12,256,4096]{2,1,0:T(8,128)} %get-tuple-element.75, f32[12,256]{1,0:T(8,128)S(1)} %log_add_fusion, bf16[256,12,64]{0,2,1:T(8,128)(2,1)S(1)} %bitcast.160, bf16[4096,12,64]{0,2,1:T(8,128)(2,1)} %reshape.271), kind=kOutput, calls=%fused_computation.2 | convolution fusion | flops 1660941312 | bytes 107372544 | tf_op jit(solution)/shard_map/while/body/eval_jaxpr/qhd,khd->hqk/dot_general | solution.py:65
  382.4 40.1 %multiply_convert_fusion = bf16[12,256,4096]{2,1,0:T(8,128)(2,1)} fusion(f32[12,256,4096]{2,1,0:T(8,128)} %get-tuple-element.80, f32[12,256,4096]{2,1,0:T(8,128)} %get-tuple-element.75, f32[12,256]{1,0:T(8,128)S(1)} %get-tuple-element.79, f32[12,256]{1,0:T(8,128)S(1)} %log_add_fusion), kind=kLoop, calls=%fused_computation.1 | loop fusion | flops 62914560 | bytes 125853696 | tf_op jit(solution)/shard_map/while/body/eval_jaxpr/convert_element_type | solution.py:69
  422.4 15.2 %multiply_convert_fusion.1 = bf16[12,64,4096]{2,1,0:T(8,128)(2,1)} fusion(bf16[256,12,64]{0,2,1:T(8,128)(2,1)S(1)} %bitcast.163, bf16[12,256,4096]{2,1,0:T(8,128)(2,1)} %multiply_convert_fusion), kind=kOutput, calls=%fused_computation.13 | convolution fusion | flops 1616904192 | bytes 31850496 | tf_op jit(solution)/shard_map/while/body/eval_jaxpr/hqk,qhd->khd/dot_general | solution.py:84
  437.8 22.1 %fusion.7 = bf16[12,64,4096]{2,1,0:T(8,128)(2,1)} fusion(bf16[256,12,64]{0,2,1:T(8,128)(2,1)S(1)} %bitcast.161, f32[12,256,4096]{2,1,0:T(8,128)} %get-tuple-element.75, f32[12,256]{1,0:T(8,128)S(1)} %log_add_fusion), kind=kOutput, calls=%fused_computation.14 | convolution fusion | flops 1651507200 | bytes 57028608 | tf_op jit(solution)/shard_map/while/body/eval_jaxpr/hqk,qhd->khd/dot_general | solution.py:87
  460.0 14.4 %fusion.18 = bf16[12,64,256]{2,1,0:T(8,128)(2,1)S(1)} fusion(bf16[4096,12,64]{0,2,1:T(8,128)(2,1)} %bitcast.157, bf16[12,256,4096]{2,1,0:T(8,128)(2,1)} %multiply_convert_fusion), kind=kOutput, calls=%fused_computation.45 | convolution fusion | flops 1611005952 | bytes 31850496 | tf_op jit(solution)/shard_map/while/body/eval_jaxpr/hqk,khd->qhd/dot_general | solution.py:74
  489.6 92.5 %reduce-scatter.10.cloned.1.call-done = bf16[1,256,768]{1,2,0:T(8,128)(2,1)} async-done(((bf16[1,4096,768]{1,2,0:T(8,128)(2,1)}), bf16[1,256,768]{1,2,0:T(8,128)(2,1)}) %reduce-scatter.10.cloned.1.call-update) | async-done | bytes 393232 | tf_op jit(solution)/shard_map/reduce_scatter | solution.py:211
  584.9 147.5 %reduce-scatter.12.cloned.1.call-done = bf16[1,256,768]{1,2,0:T(8,128)(2,1)} async-done(((bf16[1,4096,768]{1,2,0:T(8,128)(2,1)}), bf16[1,256,768]{1,2,0:T(8,128)(2,1)}) %reduce-scatter.12.cloned.1.call-update) | async-done | bytes 393232 | tf_op jit(solution)/shard_map/reduce_scatter | solution.py:214
  735.3 7.7 reduce-scatter.14.cloned.1.call-done
  743.0 12.7 %reduce-scatter.20.cloned.1.call-done = bf16[384,768]{1,0:T(8,128)(2,1)} async-done(((bf16[768,768]{1,0:T(8,128)(2,1)}), bf16[384,768]{1,0:T(8,128)(2,1)}) %reduce-scatter.20.cloned.1.call-update) | async-done | bytes 589840 | tf_op jit(solution)/shard_map/reduce_scatter | solution.py:247
  755.7 14.9 %reduce-scatter.22.cloned.1.call-done = bf16[384,2048]{1,0:T(8,128)(2,1)} async-done(((bf16[768,2048]{1,0:T(8,128)(2,1)}), bf16[384,2048]{1,0:T(8,128)(2,1)}) %reduce-scatter.22.cloned.1.call-update) | async-done | bytes 1572880 | tf_op jit(solution)/shard_map/reduce_scatter | solution.py:188
  770.6 14.9 %reduce-scatter.24.cloned.1.call-done = bf16[384,2048]{1,0:T(8,128)(2,1)} async-done(((bf16[768,2048]{1,0:T(8,128)(2,1)}), bf16[384,2048]{1,0:T(8,128)(2,1)}) %reduce-scatter.24.cloned.1.call-update) | async-done | bytes 1572880 | tf_op jit(solution)/shard_map/reduce_scatter | solution.py:191
  785.5 14.8 %reduce-scatter.26.cloned.1.call-done = bf16[1024,768]{1,0:T(8,128)(2,1)} async-done(((bf16[2048,768]{1,0:T(8,128)(2,1)}), bf16[1024,768]{1,0:T(8,128)(2,1)}) %reduce-scatter.26.cloned.1.call-update) | async-done | bytes 1572880 | tf_op jit(solution)/shard_map/reduce_scatter | solution.py:194
  800.2 12.6 %reduce-scatter.16.cloned.1.call-done = bf16[384,768]{1,0:T(8,128)(2,1)} async-done(((bf16[768,768]{1,0:T(8,128)(2,1)}), bf16[384,768]{1,0:T(8,128)(2,1)}) %reduce-scatter.16.cloned.1.call-update) | async-done | bytes 589840 | tf_op jit(solution)/shard_map/reduce_scatter | solution.py:241
  812.8 12.6 %reduce-scatter.18.cloned.1.call-done = bf16[384,768]{1,0:T(8,128)(2,1)} async-done(((bf16[768,768]{1,0:T(8,128)(2,1)}), bf16[384,768]{1,0:T(8,128)(2,1)}) %reduce-scatter.18.cloned.1.call-update) | async-done | bytes 589840 | tf_op jit(solution)/shard_map/reduce_scatter | solution.py:244
  836.2 44.0 %all-reduce.2 = (bf16[384]{0:T(512)(128)(2,1)S(1)}, bf16[384]{0:T(512)(128)(2,1)S(1)}) all-reduce(bf16[384]{0:T(512)(128)(2,1)S(1)} %dynamic-slice.3, bf16[384]{0:T(512)(128)(2,1)S(1)} %dynamic-slice.5), channel_id=1, replica_groups=mesh['dp'=2,'ctx'=16] {'ctx'}, use_global_device_ids=true, to_apply=%region_11.12 | all-reduce | flops 768 | bytes 3072 | tf_op jit(solution)/shard_map/psum | solution.py:252
  882.3 184.2 %all-reduce.7.cloned.1.call-done = (bf16[384,768]{1,0:T(8,128)(2,1)}, bf16[384,768]{1,0:T(8,128)(2,1)}, bf16[384,768]{1,0:T(8,128)(2,1)}, bf16[384,768]{1,0:T(8,...) async-done(((bf16[384,768]{1,0:T(8,128)(2,1)}, bf16[384,768]{1,0:T(8,128)(2,1)}, bf16[384,768]{1,0:T(8,128)(2,1)}, ...) | async-done | bytes 7077904 | tf_op jit(solution)/shard_map/psum | solution.py:253
  (202 shorter events, 181.9 us)
Async XLA Ops:
  7.9 25.6 %all-gather.12.cloned.1.call-start = ((), (), s32[]{:S(2)}) async-start(), calls=%async_computation.9 | async-start | bytes 1769472 | tf_op jit(solution)/shard_map/all_gather | solution.py:127
  8.7 185.7 %all-gather.14.cloned.1.call-start = ((), (), s32[]{:S(2)}) async-start(), calls=%async_computation.10 | async-start | bytes 1769472 | tf_op jit(solution)/shard_map/all_gather | solution.py:125
  9.4 246.6 %all-gather.26.cloned.1.call-start = ((), (), s32[]{:S(2)}) async-start(), calls=%async_computation.25 | async-start | bytes 6684672 | tf_op jit(solution)/shard_map/all_gather | solution.py:137
  24.2 302.6 %all-gather.18.cloned.1.call-start = ((), (), s32[]{:S(2)}) async-start(), calls=%async_computation.12 | async-start | bytes 1769472 | tf_op jit(solution)/shard_map/all_gather | solution.py:128
  24.8 304.2 %all-gather.20.cloned.1.call-start = ((), (), s32[]{:S(2)}) async-start(), calls=%async_computation.13 | async-start | bytes 4718592 | tf_op jit(solution)/shard_map/all_gather | solution.py:145
  25.4 307.9 %all-gather.22.cloned.1.call-start = ((), (), s32[]{:S(2)}) async-start(), calls=%async_computation.14 | async-start | bytes 4718592 | tf_op jit(solution)/shard_map/all_gather | solution.py:146
  26.1 311.3 %all-gather.24.cloned.1.call-start = ((), (), s32[]{:S(2)}) async-start(), calls=%async_computation.15 | async-start | bytes 4718592 | tf_op jit(solution)/shard_map/all_gather | solution.py:147
  35.3 15.0 %collective-permute-start = (bf16[1,256,768]{2,1,0:T(8,128)(2,1)S(1)}, bf16[1,256,768]{2,1,0:T(8,128)(2,1)S(1)}, u32[]{:S(2)}, u32[]{:S(2)}) collective-permute-start(bf16[1,256,768]{2,1,0:T(8,128)(2,1)S(1)} %bitcast.168), channel_id=1, source_target_pairs={{0,1},{1,2},{2,3},{3,4},{4,5},{5,6},{6,7},{7,8},{8,9},{9,10},{10,1... | collective-permute-start | bytes 1179656 | tf_op jit(solution)/shard_map/ppermute | solution.py:24
  50.3 19.6 %collective-permute-start.1 = (bf16[1,256,768]{2,1,0:T(8,128)(2,1)S(1)}, bf16[1,256,768]{2,1,0:T(8,128)(2,1)S(1)}, u32[]{:S(2)}, u32[]{:S(2)}) collective-permute-start(bf16[1,256,768]{2,1,0:T(8,128)(2,1)S(1)} %collective-permute-done), channel_id=1, source_target_pairs={{0,1},{1,2},{2,3},{3,4},{4,5},{5,6},{6,7},{7,8},{8,9},{9,10},{10,1... | collective-permute-start | bytes 1179656 | tf_op jit(solution)/shard_map/ppermute | solution.py:24
  50.3 22.1 %collective-permute-start.8 = (bf16[1,256,768]{2,1,0:T(8,128)(2,1)S(1)}, bf16[1,256,768]{2,1,0:T(8,128)(2,1)S(1)}, u32[]{:S(2)}, u32[]{:S(2)}) collective-permute-start(bf16[1,256,768]{2,1,0:T(8,128)(2,1)S(1)} %bitcast.169), channel_id=1, source_target_pairs={{1,0},{2,1},{3,2},{4,3},{5,4},{6,5},{7,6},{8,7},{9,8},{10,9},{11,1... | collective-permute-start | bytes 1179656 | tf_op jit(solution)/shard_map/ppermute | solution.py:26
  70.0 29.7 %collective-permute-start.2 = (bf16[1,256,768]{2,1,0:T(8,128)(2,1)S(1)}, bf16[1,256,768]{2,1,0:T(8,128)(2,1)S(1)}, u32[]{:S(2)}, u32[]{:S(2)}) collective-permute-start(bf16[1,256,768]{2,1,0:T(8,128)(2,1)S(1)} %collective-permute-done.1), channel_id=1, source_target_pairs={{0,1},{1,2},{2,3},{3,4},{4,5},{5,6},{6,7},{7,8},{8,9},{9,10},{10,1... | collective-permute-start | bytes 1179656 | tf_op jit(solution)/shard_map/ppermute | solution.py:24
  72.4 32.1 %collective-permute-start.9 = (bf16[1,256,768]{2,1,0:T(8,128)(2,1)S(1)}, bf16[1,256,768]{2,1,0:T(8,128)(2,1)S(1)}, u32[]{:S(2)}, u32[]{:S(2)}) collective-permute-start(bf16[1,256,768]{2,1,0:T(8,128)(2,1)S(1)} %collective-permute-done.8), channel_id=1, source_target_pairs={{1,0},{2,1},{3,2},{4,3},{5,4},{6,5},{7,6},{8,7},{9,8},{10,9},{11,1... | collective-permute-start | bytes 1179656 | tf_op jit(solution)/shard_map/ppermute | solution.py:26
  99.7 16.9 %collective-permute-start.3 = (bf16[1,256,768]{2,1,0:T(8,128)(2,1)S(1)}, bf16[1,256,768]{2,1,0:T(8,128)(2,1)S(1)}, u32[]{:S(2)}, u32[]{:S(2)}) collective-permute-start(bf16[1,256,768]{2,1,0:T(8,128)(2,1)S(1)} %collective-permute-done.2), channel_id=1, source_target_pairs={{0,1},{1,2},{2,3},{3,4},{4,5},{5,6},{6,7},{7,8},{8,9},{9,10},{10,1... | collective-permute-start | bytes 1179656 | tf_op jit(solution)/shard_map/ppermute | solution.py:24
  104.5 18.4 %collective-permute-start.10 = (bf16[1,256,768]{2,1,0:T(8,128)(2,1)S(1)}, bf16[1,256,768]{2,1,0:T(8,128)(2,1)S(1)}, u32[]{:S(2)}, u32[]{:S(2)}) collective-permute-start(bf16[1,256,768]{2,1,0:T(8,128)(2,1)S(1)} %collective-permute-done.9), channel_id=1, source_target_pairs={{1,0},{2,1},{3,2},{4,3},{5,4},{6,5},{7,6},{8,7},{9,8},{10,9},{11,1... | collective-permute-start | bytes 1179656 | tf_op jit(solution)/shard_map/ppermute | solution.py:26
  116.6 24.0 %collective-permute-start.4 = (bf16[1,256,768]{2,1,0:T(8,128)(2,1)S(1)}, bf16[1,256,768]{2,1,0:T(8,128)(2,1)S(1)}, u32[]{:S(2)}, u32[]{:S(2)}) collective-permute-start(bf16[1,256,768]{2,1,0:T(8,128)(2,1)S(1)} %collective-permute-done.3), channel_id=1, source_target_pairs={{0,1},{1,2},{2,3},{3,4},{4,5},{5,6},{6,7},{7,8},{8,9},{9,10},{10,1... | collective-permute-start | bytes 1179656 | tf_op jit(solution)/shard_map/ppermute | solution.py:24
  122.9 23.2 %collective-permute-start.11 = (bf16[1,256,768]{2,1,0:T(8,128)(2,1)S(1)}, bf16[1,256,768]{2,1,0:T(8,128)(2,1)S(1)}, u32[]{:S(2)}, u32[]{:S(2)}) collective-permute-start(bf16[1,256,768]{2,1,0:T(8,128)(2,1)S(1)} %collective-permute-done.10), channel_id=1, source_target_pairs={{1,0},{2,1},{3,2},{4,3},{5,4},{6,5},{7,6},{8,7},{9,8},{10,9},{11,1... | collective-permute-start | bytes 1179656 | tf_op jit(solution)/shard_map/ppermute | solution.py:26
  140.6 26.7 %collective-permute-start.5 = (bf16[1,256,768]{2,1,0:T(8,128)(2,1)S(1)}, bf16[1,256,768]{2,1,0:T(8,128)(2,1)}, u32[]{:S(2)}, u32[]{:S(2)}) collective-permute-start(bf16[1,256,768]{2,1,0:T(8,128)(2,1)S(1)} %collective-permute-done.4), channel_id=1, source_target_pairs={{0,1},{1,2},{2,3},{3,4},{4,5},{5,6},{6,7},{7,8},{8,9},{9,10},{10,1... | collective-permute-start | bytes 1179656 | tf_op jit(solution)/shard_map/ppermute | solution.py:24
  146.2 29.3 %collective-permute-start.12 = (bf16[1,256,768]{2,1,0:T(8,128)(2,1)S(1)}, bf16[1,256,768]{2,1,0:T(8,128)(2,1)}, u32[]{:S(2)}, u32[]{:S(2)}) collective-permute-start(bf16[1,256,768]{2,1,0:T(8,128)(2,1)S(1)} %collective-permute-done.11), channel_id=1, source_target_pairs={{1,0},{2,1},{3,2},{4,3},{5,4},{6,5},{7,6},{8,7},{9,8},{10,9},{11,1... | collective-permute-start | bytes 1179656 | tf_op jit(solution)/shard_map/ppermute | solution.py:26
  167.2 23.5 %collective-permute-start.6 = (bf16[1,256,768]{2,1,0:T(8,128)(2,1)}, bf16[1,256,768]{2,1,0:T(8,128)(2,1)}, u32[]{:S(2)}, u32[]{:S(2)}) collective-permute-start(bf16[1,256,768]{2,1,0:T(8,128)(2,1)} %collective-permute-done.5), channel_id=1, source_target_pairs={{0,1},{1,2},{2,3},{3,4},{4,5},{5,6},{6,7},{7,8},{8,9},{9,10},{10,1... | collective-permute-start | bytes 1179656 | tf_op jit(solution)/shard_map/ppermute | solution.py:24
  170.3 411.8 %reduce-scatter.10.cloned.1.call-start = ((), (), s32[]{:S(2)}) async-start(), calls=%async_computation.16 | async-start | bytes 6684672 | tf_op jit(solution)/shard_map/reduce_scatter | solution.py:211
  175.5 22.7 %collective-permute-start.13 = (bf16[1,256,768]{2,1,0:T(8,128)(2,1)}, bf16[1,256,768]{2,1,0:T(8,128)(2,1)}, u32[]{:S(2)}, u32[]{:S(2)}) collective-permute-start(bf16[1,256,768]{2,1,0:T(8,128)(2,1)} %collective-permute-done.12), channel_id=1, source_target_pairs={{1,0},{2,1},{3,2},{4,3},{5,4},{6,5},{7,6},{8,7},{9,8},{10,9},{11,1... | collective-permute-start | bytes 1179656 | tf_op jit(solution)/shard_map/ppermute | solution.py:26
  190.7 19.2 %collective-permute-start.7 = (bf16[1,256,768]{2,1,0:T(8,128)(2,1)}, bf16[1,256,768]{2,1,0:T(8,128)(2,1)}, u32[]{:S(2)}, u32[]{:S(2)}) collective-permute-start(bf16[1,256,768]{2,1,0:T(8,128)(2,1)} %collective-permute-done.6), channel_id=1, source_target_pairs={{0,1},{1,2},{2,3},{3,4},{4,5},{5,6},{6,7},{7,8},{8,9},{9,10},{10,1... | collective-permute-start | bytes 1179656 | tf_op jit(solution)/shard_map/ppermute | solution.py:24
  198.1 30.6 %collective-permute-start.14 = (bf16[1,256,768]{2,1,0:T(8,128)(2,1)}, bf16[1,256,768]{2,1,0:T(8,128)(2,1)S(1)}, u32[]{:S(2)}, u32[]{:S(2)}) collective-permute-start(bf16[1,256,768]{2,1,0:T(8,128)(2,1)} %collective-permute-done.13), channel_id=1, source_target_pairs={{1,0},{2,1},{3,2},{4,3},{5,4},{6,5},{7,6},{8,7},{9,8},{10,9},{11,1... | collective-permute-start | bytes 1179656 | tf_op jit(solution)/shard_map/ppermute | solution.py:26
  437.7 294.7 %reduce-scatter.12.cloned.1.call-start = ((), (), s32[]{:S(2)}) async-start(), calls=%async_computation.17 | async-start | bytes 6684672 | tf_op jit(solution)/shard_map/reduce_scatter | solution.py:214
  459.9 283.1 %reduce-scatter.14.cloned.1.call-start = ((), (), s32[]{:S(2)}) async-start(), calls=%async_computation.18 | async-start | bytes 1769472 | tf_op jit(solution)/shard_map/reduce_scatter | solution.py:238
  476.1 279.6 %reduce-scatter.20.cloned.1.call-start = ((), (), s32[]{:S(2)}) async-start(), calls=%async_computation.21 | async-start | bytes 1769472 | tf_op jit(solution)/shard_map/reduce_scatter | solution.py:247
  478.7 291.9 %reduce-scatter.22.cloned.1.call-start = ((), (), s32[]{:S(2)}) async-start(), calls=%async_computation.22 | async-start | bytes 4718592 | tf_op jit(solution)/shard_map/reduce_scatter | solution.py:188
  482.7 302.8 %reduce-scatter.24.cloned.1.call-start = ((), (), s32[]{:S(2)}) async-start(), calls=%async_computation.23 | async-start | bytes 4718592 | tf_op jit(solution)/shard_map/reduce_scatter | solution.py:191
  485.5 314.8 %reduce-scatter.26.cloned.1.call-start = ((), (), s32[]{:S(2)}) async-start(), calls=%async_computation.24 | async-start | bytes 4718592 | tf_op jit(solution)/shard_map/reduce_scatter | solution.py:194
  489.6 323.3 %reduce-scatter.16.cloned.1.call-start = ((), (), s32[]{:S(2)}) async-start(), calls=%async_computation.19 | async-start | bytes 1769472 | tf_op jit(solution)/shard_map/reduce_scatter | solution.py:241
  584.8 240.6 %reduce-scatter.18.cloned.1.call-start = ((), (), s32[]{:S(2)}) async-start(), calls=%async_computation.20 | async-start | bytes 1769472 | tf_op jit(solution)/shard_map/reduce_scatter | solution.py:244
  735.0 331.5 %all-reduce.7.cloned.1.call-start = ((), (), s32[]{:S(2)}) async-start(), calls=%async_computation.26 | async-start | bytes 14155776 | tf_op jit(solution)/shard_map/psum | solution.py:253
  (34 other events, 1906.1 us)
Sparse Core Ops, SparseCore 0:
  9.6 11.9 all-gather.15
  23.1 10.3 all-gather.11
  35.0 10.3 all-gather.13
  48.7 146.7 all-gather.25
  196.9 18.6 all-gather.17
  216.9 13.2 all-gather.19
  231.8 13.2 all-gather.21
  246.7 13.2 all-gather.23
  437.8 144.2 reduce-scatter.9
  587.2 145.1 reduce-scatter.11
  735.2 7.7 reduce-scatter.13
  745.8 9.8 reduce-scatter.19
  758.5 12.0 reduce-scatter.21
  773.4 12.0 reduce-scatter.23
  788.1 12.0 reduce-scatter.25
  803.0 9.8 reduce-scatter.15
  815.5 9.8 reduce-scatter.17
  832.8 233.6 all-reduce.6
